TPU v7x, 32 devices: a whole 2x2x4 slice. The times are simulated.
32 devices in a mesh: row: 4 (over y, x), col: 8 (over z, core).
Axes of the slice: x: 2, y: 2, z: 4, core: 2. Of those that a mesh axis runs over, the one named last changes fastest.
Arguments:
- right_side: float32 [512, 128], P('row'), may hold values from -6 to 6
- factor_window: float32 [512, 512], P('row', 'col'), may hold values from -0.1875 to 0.1875
- diag_inverse: float32 [512, 128], P('row'), as said below
- phase_cov: bfloat16 [512, 16384], P('col', 'row'), may hold values from -0.25 to 0.25
Outputs:
- basis: float32 [32, 512, 128], P('row', 'col')
- solved: float32 [512, 128], P('col')
Inputs may be any that keep to these rules, and one draw needn't show every extreme that they name: `diag_inverse`: each block of 128 rows is a lower triangular matrix with a diagonal between 0.5 and 2.
All inputs are finite; a program needn't handle non-finite values.
Results may differ from a plain program's by a relative error of at most 0.0043.
Values sent between devices are 32-bit elements; how exact they have to be, the bound alone decides.
A program may use at most 64 MiB of HBM per device.

v0:
```python
import jax
import jax.numpy as jnp
from jax import lax
from jax.sharding import PartitionSpec as P

TILE_ROWS = 512


def from_root(block, axis, owner):
    block = jnp.where(lax.axis_index(axis) == owner, block, jnp.zeros_like(block))
    return lax.psum(block, axis)


def tile_basis(lower, tile):
    return jax.scipy.linalg.solve_triangular(lower, tile.T, lower=True).T


def finish_tiles(gram, tiles):
    lower = jnp.linalg.cholesky(gram)
    return jax.vmap(tile_basis)(lower, tiles)


def local(right_side, factor_window, diag_inverse, phase_cov):
    row_count = lax.axis_size("row")
    col_count = lax.axis_size("col")
    col_index = lax.axis_index("col")
    block_rows = right_side.shape[0]
    rank_width = right_side.shape[1]
    col_width = factor_window.shape[1]
    col_ratio = col_count // row_count
    row_offset = col_index % col_ratio * col_width
    owner_block = col_index // col_ratio
    partial_value = jnp.zeros((block_rows, rank_width), jnp.float32)
    own_solved = jnp.zeros((col_width, rank_width), jnp.float32)
    for block_index in range(row_count):
        summed = lax.psum(partial_value, "col")
        remaining = right_side - summed
        solved_full = jnp.dot(
            diag_inverse,
            remaining,
            precision=lax.Precision.HIGHEST,
            preferred_element_type=jnp.float32,
        )
        received = from_root(solved_full, "row", block_index)
        column_piece = lax.dynamic_slice_in_dim(received, row_offset, col_width, 0)
        owns_block = owner_block == block_index
        own_solved = jnp.where(owns_block, column_piece, own_solved)
        partial_value = lax.cond(
            owns_block,
            lambda running: running
            + jnp.dot(
                factor_window,
                column_piece,
                precision=lax.Precision.HIGHEST,
                preferred_element_type=jnp.float32,
            ),
            lambda running: running,
            partial_value,
        )
    solved_low = own_solved.astype(jnp.bfloat16)
    tile_count = phase_cov.shape[1] // TILE_ROWS
    cov_tiles = phase_cov.reshape(col_width, tile_count, TILE_ROWS)
    whole_tiles = lax.psum_scatter(
        jnp.einsum("kts,kr->tsr", cov_tiles, solved_low, preferred_element_type=jnp.float32),
        "col",
        scatter_dimension=0,
        tiled=True,
    )
    gram = jnp.einsum("tsr,tsq->trq", whole_tiles, whole_tiles, precision=lax.Precision.HIGHEST)
    tile_bases = finish_tiles(gram, whole_tiles)
    basis = lax.all_to_all(tile_bases, "col", split_axis=1, concat_axis=0, tiled=True)
    return (basis, own_solved)


def solution(mesh):
    in_specs = (P("row", None), P("row", "col"), P("row", None), P("col", "row"))
    out_specs = (P("row", "col", None), P("col", None))
    return jax.shard_map(local, mesh=mesh, in_specs=in_specs, out_specs=out_specs, check_vma=False)
```

profile of v0, /device:TPU:0, one launch (start us, length us, event | category | flops | bytes accessed | tf_op | source)
XLA Modules:
  0.0 444.9 jit_solution(12275134099939349102)
XLA Ops:
  7.2 0.0 copy-start
  7.2 0.0 all-reduce.8.cloned.1.call-start
  7.2 0.8 copy-done
  8.0 1.7 convolution_select_fusion.3
  9.7 0.0 all-reduce.8.cloned.1.call-update
  9.7 0.0 all-reduce.10.cloned.1.call-start
  9.8 46.2 %all-reduce.8.cloned.1.call-done = f32[128,128]{1,0:T(8,128)} async-done(((f32[128,128]{1,0:T(8,128)}), f32[128,128]{1,0:T(8,128)}) %all-reduce.8.cloned.1.call-update) | async-done | bytes 65552 | tf_op jit(solution)/shard_map/psum | solution.py:11
  56.0 0.8 constant_dynamic-slice_fusion.2
  56.8 1.0 conditional.3
  56.8 1.0 fusion.16
  57.8 0.6 copy-done.1
  58.5 0.0 all-reduce.10.cloned.1.call-update
  58.5 0.0 all-reduce.12.cloned.1.call-start
  58.5 55.1 %all-reduce.10.cloned.1.call-done = f32[128,128]{1,0:T(8,128)} async-done(((f32[128,128]{1,0:T(8,128)}), f32[128,128]{1,0:T(8,128)}) %all-reduce.10.cloned.1.call-update) | async-done | bytes 65552 | tf_op jit(solution)/shard_map/psum | solution.py:36
  113.6 1.7 fusion.2
  115.3 0.0 all-reduce.12.cloned.1.call-update
  115.4 0.0 all-reduce.14.cloned.1.call-start
  115.4 42.0 %all-reduce.12.cloned.1.call-done = f32[128,128]{1,0:T(8,128)} async-done(((f32[128,128]{1,0:T(8,128)}), f32[128,128]{1,0:T(8,128)}) %all-reduce.12.cloned.1.call-update) | async-done | bytes 65552 | tf_op jit(solution)/shard_map/psum | solution.py:11
  157.4 0.8 constant_dynamic-slice_fusion.1
  158.2 0.0 all-reduce.14.cloned.1.call-update
  158.2 0.0 all-reduce.16.cloned.1.call-start
  158.2 56.6 %all-reduce.14.cloned.1.call-done = f32[128,128]{1,0:T(8,128)} async-done(((f32[128,128]{1,0:T(8,128)}), f32[128,128]{1,0:T(8,128)}) %all-reduce.14.cloned.1.call-update) | async-done | bytes 65552 | tf_op jit(solution)/shard_map/psum | solution.py:36
  214.9 1.7 fusion.1
  216.6 0.0 all-reduce.16.cloned.1.call-update
  216.6 0.0 all-reduce.18.cloned.1.call-start
  216.7 41.8 %all-reduce.16.cloned.1.call-done = f32[128,128]{1,0:T(8,128)} async-done(((f32[128,128]{1,0:T(8,128)}), f32[128,128]{1,0:T(8,128)}) %all-reduce.16.cloned.1.call-update) | async-done | bytes 65552 | tf_op jit(solution)/shard_map/psum | solution.py:11
  258.5 0.8 constant_dynamic-slice_fusion
  259.3 0.0 all-reduce.18.cloned.1.call-update
  259.3 0.0 all-reduce.20.cloned.1.call-start
  259.3 56.6 %all-reduce.18.cloned.1.call-done = f32[128,128]{1,0:T(8,128)} async-done(((f32[128,128]{1,0:T(8,128)}), f32[128,128]{1,0:T(8,128)}) %all-reduce.18.cloned.1.call-update) | async-done | bytes 65552 | tf_op jit(solution)/shard_map/psum | solution.py:36
  316.0 1.7 fusion
  317.7 0.0 all-reduce.20.cloned.1.call-update
  317.7 0.0 reduce-scatter.2.cloned.1.call-start
  317.8 42.6 %all-reduce.20.cloned.1.call-done = f32[128,128]{1,0:T(8,128)} async-done(((f32[128,128]{1,0:T(8,128)}), f32[128,128]{1,0:T(8,128)}) %all-reduce.20.cloned.1.call-update) | async-done | bytes 65552 | tf_op jit(solution)/shard_map/psum | solution.py:11
  360.3 0.8 select_select_fusion.1
  361.2 1.8 convolution_bitcast_fusion
  362.9 0.0 reduce-scatter.2.cloned.1.call-update
  363.0 36.4 %reduce-scatter.2.cloned.1.call-done = f32[1,512,128]{1,2,0:T(8,128)} async-done(((f32[8,512,128]{1,2,0:T(8,128)}), f32[1,512,128]{1,2,0:T(8,128)}) %reduce-scatter.2.cloned.1.call-update) | async-done | bytes 262160 | tf_op jit(solution)/shard_map/reduce_scatter | solution.py:63
  399.3 1.4 fusion.6
  400.8 0.1 copy.37
  400.9 11.7 %custom-call.8 = f32[1,128,128]{2,1,0:T(8,128)S(1)} custom-call(f32[1,128,128]{2,1,0:T(8,128)S(1)} %fusion.9), custom_call_target="Cholesky" | custom-call | tf_op jit(solution)/shard_map/jit(cholesky)/cholesky | solution.py:19
  412.6 0.6 compare_reduce_fusion
  413.3 0.7 fusion.8
  413.9 9.8 %custom-call.9 = f32[1,1,128,128]{2,3,1,0:T(8,128)S(1)} custom-call(f32[1,1,128,128]{3,2,1,0:T(8,128)S(1)} %fusion.8), custom_call_target="InvertDiagBlocksLowerTriangular" | custom-call | tf_op jit(solution)/shard_map/vmap(jit(_solve_triangular))/triangular_solve | solution.py:15
  423.7 1.4 convolution_bitcast_fusion.1
  425.1 0.1 copy.38
  425.2 12.1 %all_to_all.12 = f32[1,512,128]{2,0,1:T(1,128)S(1)} all-to-all(f32[1,512,128]{2,0,1:T(1,128)S(1)} %copy.38), channel_id=1, replica_groups=mesh['row'=4,'col'=8] {'col'}, dimensions={1} | all-to-all | bytes 524288 | tf_op jit(solution)/shard_map/all_to_all | solution.py:71
  437.4 0.7 copy.66
  (9 shorter events, 0.1 us)
Async XLA Ops:
  7.2 0.8 copy-start
  7.2 354.0 %copy-start.2 = (bf16[64,4096]{1,0:T(8,128)(2,1)S(1)}, bf16[64,4096]{1,0:T(8,128)(2,1)}, u32[]{:S(2)}) copy-start(bf16[64,4096]{1,0:T(8,128)(2,1)} %param.13) | copy-start | bytes 1572868
  7.2 48.8 %all-reduce.8.cloned.1.call-start = ((), (), s32[]{:S(2)}) async-start(), calls=%async_computation.2 | async-start | bytes 131072 | tf_op jit(solution)/shard_map/psum | solution.py:11
  9.7 103.9 %all-reduce.10.cloned.1.call-start = ((), (), s32[]{:S(2)}) async-start(), calls=%async_computation.3 | async-start | bytes 131072 | tf_op jit(solution)/shard_map/psum | solution.py:36
  57.8 0.6 copy-start.1
  58.5 98.9 %all-reduce.12.cloned.1.call-start = ((), (), s32[]{:S(2)}) async-start(), calls=%async_computation.4 | async-start | bytes 131072 | tf_op jit(solution)/shard_map/psum | solution.py:11
  115.4 99.5 %all-reduce.14.cloned.1.call-start = ((), (), s32[]{:S(2)}) async-start(), calls=%async_computation.5 | async-start | bytes 131072 | tf_op jit(solution)/shard_map/psum | solution.py:36
  158.2 100.3 %all-reduce.16.cloned.1.call-start = ((), (), s32[]{:S(2)}) async-start(), calls=%async_computation.6 | async-start | bytes 131072 | tf_op jit(solution)/shard_map/psum | solution.py:11
  216.6 99.4 %all-reduce.18.cloned.1.call-start = ((), (), s32[]{:S(2)}) async-start(), calls=%async_computation.7 | async-start | bytes 131072 | tf_op jit(solution)/shard_map/psum | solution.py:36
  259.3 101.0 %all-reduce.20.cloned.1.call-start = ((), (), s32[]{:S(2)}) async-start(), calls=%async_computation.8 | async-start | bytes 131072 | tf_op jit(solution)/shard_map/psum | solution.py:11
  317.7 81.6 %reduce-scatter.2.cloned.1.call-start = ((), (), s32[]{:S(2)}) async-start(), calls=%async_computation.9 | async-start | bytes 2359296 | tf_op jit(solution)/shard_map/reduce_scatter | solution.py:63
  361.1 1.8 copy-start.3
Sparse Core Ops, SparseCore 0:
  11.4 44.5 all-reduce.7
  58.9 54.6 all-reduce.9
  116.5 40.8 all-reduce.11
  160.1 54.6 all-reduce.13
  217.6 40.8 all-reduce.15
  261.2 54.6 all-reduce.17
  319.4 40.8 all-reduce.19
  363.1 36.2 reduce-scatter.1
where the time goes:
time: 446 us; the launch traced here: 445 us
  waiting for transfers between devices  377 us (85%)
  other arithmetic  23.7 us (5%)
  between operations  14.3 us (3%)
  matrix products  12.4 us (3%)
  blocking collectives  12.1 us (3%)
  local copies, waits for them, and re-layouts  4.6 us (1%)
    psum x4, waiting for transfers between devices, from_root(): return lax.psum(block, axis)  173 us
    psum x3, waiting for transfers between devices, local(): summed = lax.psum(partial_value, 'col')  168 us
    reduce_scatter x1, waiting for transfers between devices, local(): lax.psum_scatter(jnp.einsum('kts,kr->tsr', cov_tiles, solved_low, preferr...  36.4 us
    another operation x3, other arithmetic, finish_tiles(): lower = jnp.linalg.cholesky(gram)  12.4 us
    all_to_all x1, blocking collectives, local(): lax.all_to_all(tile_bases, 'col', split_axis=1, concat_axis=0, tiled=True)  12.1 us
    another operation x2, other arithmetic, tile_basis(): return jax.scipy.linalg.solve_triangular(lower, tile.T, lower=True).T  10.5 us
  transfers between devices with their start and end apart: 8, of which 8 were waited for; matrix products, arithmetic and copies ran while one was open for 0% of the time, Pallas kernels for 0%

commit v1 on v0

v1 whole, which is shorter than its diff:
```python
import functools

import jax
import jax.numpy as jnp
from jax import lax
from jax.experimental import pallas as pl
from jax.experimental.pallas import tpu as pltpu
from jax.sharding import PartitionSpec as P

MESH = pl.DeviceIdType.MESH
CORES = 2
SUB = 8
F32 = jnp.float32
dot_exact = functools.partial(lax.dot_general, precision=lax.Precision.HIGHEST, preferred_element_type=F32)
NN = (((1,), (0,)), ((), ()))
NT = (((1,), (1,)), ((), ()))


def factor_inverse(gram):
    size = gram.shape[0]
    groups = size // SUB
    parts = [gram[g * SUB:(g + 1) * SUB, :] for g in range(groups)]
    lane = lax.broadcasted_iota(jnp.int32, (SUB, size), 1)
    sub = lax.broadcasted_iota(jnp.int32, (SUB, size), 0)
    pivots = [None] * groups
    for k in range(size):
        g0, k0 = divmod(k, SUB)
        at_k = lane == k
        cols = [jnp.broadcast_to(parts[g][:, k:k + 1], (SUB, size)) for g in range(g0, groups)]
        pivot = jnp.broadcast_to(cols[0][k0:k0 + 1, :], (SUB, size))
        row = jnp.broadcast_to(parts[g0][k0:k0 + 1, :], (SUB, size))
        inverse = 1.0 / pivot
        scaled = jnp.where(at_k, inverse, row * inverse)
        pivots[g0] = pivot if k0 == 0 else jnp.where(sub >= k0, pivot, pivots[g0])
        for g in range(g0, groups):
            updated = jnp.where(at_k, 0.0, parts[g]) - cols[g - g0] * scaled
            parts[g] = jnp.where(sub > k0, updated, parts[g]) if g == g0 else updated
    out = []
    for g in range(groups):
        below = jnp.where(lane < sub + g * SUB, parts[g], jnp.where(lane == sub + g * SUB, 1.0, 0.0))
        out.append(below * lax.rsqrt(pivots[g]))
    return jnp.concatenate(out, axis=0)


def kernel(n_row, n_col, rs_ref, fw_ref, di_ref, cov_ref, basis_ref, solved_ref,
           cov32, tile, rows, solved_all, bases,
           cov_send, cov_recv, f_send, f_fwd, f_recv, x_send, x_recv, b_send, b_recv):
    row = lax.axis_index("row")
    col = lax.axis_index("col")
    chips = n_col // CORES
    chip, core = col // CORES, col % CORES
    partner = chip * CORES + (1 - core)
    block = rs_ref.shape[0]
    width = fw_ref.shape[1]
    piece = cov32.shape[2]
    out_rows = bases.shape[1]

    barrier = pltpu.get_barrier_semaphore()
    for d in range(1, n_row):
        pl.semaphore_signal(barrier, inc=1, device_id=(lax.rem(row + d, n_row), col), device_id_type=MESH)
    for d in range(1, n_col):
        pl.semaphore_signal(barrier, inc=1, device_id=(row, lax.rem(col + d, n_col)), device_id_type=MESH)

    di = di_ref[...]
    rows[row, pl.ds(0, block), :] = dot_exact(rs_ref[...].T, di, NT)
    rows[row, pl.ds(block + col * width, width), :] = dot_exact(fw_ref[...].T, di, NT)
    for t in range(n_col):
        cov32[t] = cov_ref[:, t * piece:(t + 1) * piece].astype(F32)
    pl.semaphore_wait(barrier, n_row + n_col - 2)

    def f_copy(source, target, send):
        view = rows.at[row, pl.ds(block + source * width, width)]
        return pltpu.make_async_remote_copy(
            src_ref=view, dst_ref=view, send_sem=send, recv_sem=f_recv.at[source],
            device_id=(row, target), device_id_type=MESH)

    def far(d):
        return lax.rem(chip + d, chips) * CORES + core

    f_sends = [f_copy(col, far(d), f_send.at[d]) for d in range(1, chips)]
    f_sends.append(f_copy(col, partner, f_send.at[0]))
    for copy in f_sends:
        copy.start()

    def cov_copy(source, target, d):
        return pltpu.make_async_remote_copy(
            src_ref=cov32.at[target], dst_ref=tile.at[source],
            send_sem=cov_send.at[d], recv_sem=cov_recv.at[source],
            device_id=(row, target), device_id_type=MESH)

    order = sorted(range(1, n_col), key=lambda d: abs(2 * d - n_col))
    cov_sends = [cov_copy(col, lax.rem(col + d, n_col), d) for d in order]
    for copy in cov_sends:
        copy.start()
    tile[col] = cov32[col]

    forwards = []
    for d in range(1, chips):
        source = far(d)
        f_copy(source, partner, f_fwd.at[d]).wait_recv()
        copy = f_copy(source, partner, f_fwd.at[d])
        copy.start()
        forwards.append(copy)
    for d in range(chips):
        source = lax.rem(chip + d, chips) * CORES + (1 - core)
        f_copy(source, partner, f_fwd.at[0]).wait_recv()

    def x_copy(i, target, d):
        view = rows.at[i, pl.ds(0, (i + 1) * block)]
        return pltpu.make_async_remote_copy(
            src_ref=view, dst_ref=view, send_sem=x_send.at[d], recv_sem=x_recv.at[i],
            device_id=(target, col), device_id_type=MESH)

    for i in range(n_row):
        @pl.when(row == i)
        def _():
            for d in range(1, n_row):
                x_copy(i, (i + d) % n_row, d).start()

    solved = []
    for i in range(n_row):
        @pl.when(row != i)
        def _():
            x_copy(i, (i + 1) % n_row, 0).wait_recv()

        value = rows[i, pl.ds(0, block), :]
        if i:
            earlier = jnp.concatenate(solved, axis=1) if i > 1 else solved[0]
            value = value - dot_exact(earlier, rows[i, pl.ds(block, i * block), :], NN)
        solved.append(value)
        solved_all[pl.ds(i * block, block), :] = value.T
    solved_low = jnp.concatenate(solved, axis=1).astype(jnp.bfloat16)
    solved_ref[...] = solved_all[pl.ds(pl.multiple_of(col * width, width), width), :]

    for d in order:
        cov_copy(lax.rem(col + d, n_col), col, d).wait_recv()
    whole = tile[...].reshape(n_col * width, piece).astype(jnp.bfloat16)
    weighted = lax.dot_general(solved_low, whole, NN, preferred_element_type=F32)
    inverse = factor_inverse(dot_exact(weighted, weighted, NT))
    basis = dot_exact(weighted.T, inverse, NT)
    bases[...] = basis.reshape(bases.shape)

    def b_copy(source, target, d):
        return pltpu.make_async_remote_copy(
            src_ref=bases.at[target], dst_ref=basis_ref.at[source],
            send_sem=b_send.at[d], recv_sem=b_recv.at[source],
            device_id=(row, target), device_id_type=MESH)

    b_sends = [b_copy(col, lax.rem(col + d, n_col), d) for d in order]
    for copy in b_sends:
        copy.start()
    basis_ref[col] = bases[col]
    for copy in f_sends + forwards + cov_sends:
        copy.wait_send()
    for i in range(n_row):
        @pl.when(row == i)
        def _():
            for d in range(1, n_row):
                x_copy(i, (i + d) % n_row, d).wait_send()
    for d in order:
        b_copy(lax.rem(col + d, n_col), col, d).wait_recv()
    for copy in b_sends:
        copy.wait_send()


def solution(mesh):
    n_row, n_col = mesh.shape["row"], mesh.shape["col"]

    def local(right_side, factor_window, diag_inverse, phase_cov):
        block, rank = right_side.shape
        width = factor_window.shape[1]
        piece = phase_cov.shape[1] // n_col
        out_rows = piece // n_col
        vmem = pl.BlockSpec(memory_space=pltpu.VMEM)
        dma = pltpu.SemaphoreType.DMA
        return pl.pallas_call(
            functools.partial(kernel, n_row, n_col),
            out_shape=(
                jax.ShapeDtypeStruct((n_col, out_rows, rank), F32),
                jax.ShapeDtypeStruct((width, rank), F32),
            ),
            in_specs=[vmem] * 4,
            out_specs=(vmem, vmem),
            scratch_shapes=[
                pltpu.VMEM((n_col, width, piece), F32),
                pltpu.VMEM((n_col, width, piece), F32),
                pltpu.VMEM((n_row, (n_row + 1) * block, rank), F32),
                pltpu.VMEM((n_row * block, rank), F32),
                pltpu.VMEM((n_col, out_rows, rank), F32),
                dma((n_col,)), dma((n_col,)),
                dma((n_col,)), dma((n_col,)), dma((n_col,)),
                dma((n_row,)), dma((n_row,)),
                dma((n_col,)), dma((n_col,)),
            ],
            compiler_params=pltpu.CompilerParams(collective_id=0, has_side_effects=True),
        )(right_side, factor_window, diag_inverse, phase_cov)

    in_specs = (P("row", None), P("row", "col"), P("row", None), P("col", "row"))
    out_specs = (P("row", "col", None), P("col", None))
    return jax.shard_map(local, mesh=mesh, in_specs=in_specs, out_specs=out_specs, check_vma=False)
```

time: 446 us -> 61 us (0.14)
  waiting for transfers between devices: 377 us -> 0 us
  Pallas kernels: 0 us -> 56.3 us
  other arithmetic: 23.7 us -> 0 us
  between operations: 14.3 us -> 0.65 us
  matrix products: 12.4 us -> 0 us
  blocking collectives: 12.1 us -> 0 us
    psum x7 -> x0, waiting for transfers between devices: 341 us -> none  [the longest x4 173 us: from_root(): return lax.psum(block, axis)]
    pallas_call x0 -> x1, Pallas kernels: none -> 56.3 us  [local(): pl.pallas_call(functools.partial(kernel, n_row, n_col), out_shape=(jax.Sh...]
    reduce_scatter x1 -> x0, waiting for transfers between devices: 36.4 us -> none  [local(): lax.psum_scatter(jnp.einsum('kts,kr->tsr', cov_tiles, solved_low, preferr...]
    another operation x5 -> x0, other arithmetic: 22.9 us -> none  [the longest x3 12.4 us: finish_tiles(): lower = jnp.linalg.cholesky(gram)]
    all_to_all x1 -> x0, blocking collectives: 12.1 us -> none  [local(): lax.all_to_all(tile_bases, 'col', split_axis=1, concat_axis=0, tiled=True)]
    dot_general x7 -> x0, matrix products: 11 us -> none  [the longest x4 6.8 us: local(): jnp.dot(diag_inverse, remaining, precision=lax.Precision.HIGHEST, preferr...]
  transfers between devices with their start and end apart: 8 -> 0, of which waited for: 8 -> 0; matrix products, arithmetic and copies ran while one was open for 0% -> 0% of each run, Pallas kernels for 0% -> 0%
where the time goes in v1:
time: 61 us; the launch traced here: 60.8 us
  Pallas kernels  56.3 us (92%)
  local copies, waits for them, and re-layouts  3.78 us (6%)
  between operations  0.65 us (1%)
    pallas_call x1, Pallas kernels, local(): pl.pallas_call(functools.partial(kernel, n_row, n_col), out_shape=(jax.Sh...  56.3 us
    unnamed x5, local copies, waits for them, and re-layouts  3.78 us

profile of v1, /device:TPU:0, one launch (start us, length us, event | category | flops | bytes accessed | tf_op | source)
XLA Modules:
  0.0 60.8 jit_solution(2280161719370158541)
XLA Ops:
  0.6 1.5 %copy.6.fw_ref = f32[128,64]{1,0:T(8,128)} copy(f32[128,64]{0,1:T(8,128)} %param.5) | data formatting | bytes 65536 | tf_op args[1]
  2.1 56.3 %shard_map.59 = (f32[8,64,128]{2,1,0:T(8,128)}, f32[64,128]{1,0:T(8,128)}) custom-call(f32[128,128]{1,0:T(8,128)} %rs_ref.1, f32[128,64]{1,0:T(8,128)} %copy.6.fw_ref, f32[128,128]{1,0:T(8,128)} %di_ref.1, bf16[64,4096]{1,0:T(8,128)(2,1)} %cov_ref.1), custom_call_target="tpu_custom_call" | custom-call | tf_op jit(solution)/shard_map/pallas_call | solution.py:176
  58.5 0.0 copy-start
  58.5 1.7 %copy.9 = f32[8,64,128]{2,1,0:T(8,128)} copy(f32[8,64,128]{2,1,0:T(8,128)} %get-tuple-element.4) | data formatting | bytes 524288
  60.1 0.0 copy-done
  60.2 0.6 %copy.10 = f32[64,128]{1,0:T(8,128)} copy(f32[64,128]{1,0:T(8,128)S(1)} %copy-done) | data formatting | bytes 65536
Async XLA Ops:
  58.5 1.7 %copy-start = (f32[64,128]{1,0:T(8,128)S(1)}, f32[64,128]{1,0:T(8,128)}, u32[]{:S(2)}) copy-start(f32[64,128]{1,0:T(8,128)} %get-tuple-element.5) | copy-start | bytes 98308

commit v2 on v1

--- a/solution.py
+++ b/solution.py
@@ -22,23 +22,38 @@
     parts = [gram[g * SUB:(g + 1) * SUB, :] for g in range(groups)]
     lane = lax.broadcasted_iota(jnp.int32, (SUB, size), 1)
     sub = lax.broadcasted_iota(jnp.int32, (SUB, size), 0)
-    pivots = [None] * groups
-    for k in range(size):
-        g0, k0 = divmod(k, SUB)
-        at_k = lane == k
-        cols = [jnp.broadcast_to(parts[g][:, k:k + 1], (SUB, size)) for g in range(g0, groups)]
-        pivot = jnp.broadcast_to(cols[0][k0:k0 + 1, :], (SUB, size))
-        row = jnp.broadcast_to(parts[g0][k0:k0 + 1, :], (SUB, size))
-        inverse = 1.0 / pivot
-        scaled = jnp.where(at_k, inverse, row * inverse)
-        pivots[g0] = pivot if k0 == 0 else jnp.where(sub >= k0, pivot, pivots[g0])
-        for g in range(g0, groups):
-            updated = jnp.where(at_k, 0.0, parts[g]) - cols[g - g0] * scaled
-            parts[g] = jnp.where(sub > k0, updated, parts[g]) if g == g0 else updated
+    spread = lambda x: jnp.broadcast_to(x, (SUB, size))
     out = []
-    for g in range(groups):
-        below = jnp.where(lane < sub + g * SUB, parts[g], jnp.where(lane == sub + g * SUB, 1.0, 0.0))
-        out.append(below * lax.rsqrt(pivots[g]))
+    for g0 in range(groups):
+        base = g0 * SUB
+        inside = (lane >= base) & (lane < base + SUB)
+        cols = [spread(parts[g0][:, base + j:base + j + 1]) for j in range(SUB)]
+        entry = {(i, j): spread(cols[j][i:i + 1, :]) for i in range(SUB) for j in range(i + 1)}
+        lines = [jnp.where(inside, jnp.where(lane == base + j, 1.0, 0.0), spread(parts[g0][j:j + 1, :])) for j in range(SUB)]
+        ratio, inverses = {}, []
+        for j in range(SUB):
+            inverse = 1.0 / entry[j, j]
+            inverses.append(inverse)
+            for l in range(j + 1, SUB):
+                ratio[l, j] = entry[l, j] * inverse
+            for l in range(j + 1, SUB):
+                for i in range(l, SUB):
+                    entry[i, l] = entry[i, l] - entry[i, j] * ratio[l, j]
+                lines[l] = lines[l] - ratio[l, j] * lines[j]
+        scaled = [lines[j] * inverses[j] for j in range(SUB)]
+        for g in range(g0 + 1, groups):
+            left = [spread(parts[g][:, base + j:base + j + 1]) for j in range(SUB)]
+            value = jnp.where(inside, 0.0, parts[g])
+            for j in range(SUB):
+                for l in range(j + 1, SUB):
+                    left[l] = left[l] - left[j] * ratio[l, j]
+                value = value - left[j] * scaled[j]
+            parts[g] = value
+        done, pivot = lines[0], entry[0, 0]
+        for j in range(1, SUB):
+            done = jnp.where(sub == j, lines[j], done)
+            pivot = jnp.where(sub == j, entry[j, j], pivot)
+        out.append(jnp.where(lane <= sub + base, done * lax.rsqrt(pivot), 0.0))
     return jnp.concatenate(out, axis=0)
 
 
@@ -51,9 +66,8 @@
     chip, core = col // CORES, col % CORES
     partner = chip * CORES + (1 - core)
     block = rs_ref.shape[0]
-    width = fw_ref.shape[1]
+    width = fw_ref.shape[0]
     piece = cov32.shape[2]
-    out_rows = bases.shape[1]
 
     barrier = pltpu.get_barrier_semaphore()
     for d in range(1, n_row):
@@ -63,7 +77,7 @@
 
     di = di_ref[...]
     rows[row, pl.ds(0, block), :] = dot_exact(rs_ref[...].T, di, NT)
-    rows[row, pl.ds(block + col * width, width), :] = dot_exact(fw_ref[...].T, di, NT)
+    rows[row, pl.ds(block + col * width, width), :] = dot_exact(fw_ref[...], di, NT)
     for t in range(n_col):
         cov32[t] = cov_ref[:, t * piece:(t + 1) * piece].astype(F32)
     pl.semaphore_wait(barrier, n_row + n_col - 2)
@@ -176,8 +190,8 @@
         return pl.pallas_call(
             functools.partial(kernel, n_row, n_col),
             out_shape=(
-                jax.ShapeDtypeStruct((n_col, out_rows, rank), F32),
-                jax.ShapeDtypeStruct((width, rank), F32),
+                pltpu.VMEM((n_col, out_rows, rank), F32),
+                pltpu.VMEM((width, rank), F32),
             ),
             in_specs=[vmem] * 4,
             out_specs=(vmem, vmem),
@@ -193,7 +207,7 @@
                 dma((n_col,)), dma((n_col,)),
             ],
             compiler_params=pltpu.CompilerParams(collective_id=0, has_side_effects=True),
-        )(right_side, factor_window, diag_inverse, phase_cov)
+        )(right_side, factor_window.T, diag_inverse, phase_cov)
 
     in_specs = (P("row", None), P("row", "col"), P("row", None), P("col", "row"))
     out_specs = (P("row", "col", None), P("col", None))

time: 61 us -> 44.8 us (0.73)
  Pallas kernels: 56.3 us -> 42.7 us
  local copies, waits for them, and re-layouts: 3.78 us -> 1.32 us
    pallas_call x1, Pallas kernels: 56.3 us -> 42.7 us  [local(): pl.pallas_call(functools.partial(kernel, n_row, n_col), out_shape=(pltpu....]
    unnamed x5 -> x2, local copies, waits for them, and re-layouts: 3.78 us -> 1.32 us
where the time goes in v2:
time: 44.8 us; the launch traced here: 44.7 us
  Pallas kernels  42.7 us (95%)
  local copies, waits for them, and re-layouts  1.32 us (3%)
  between operations  0.64 us (1%)
    pallas_call x1, Pallas kernels, local(): pl.pallas_call(functools.partial(kernel, n_row, n_col), out_shape=(pltpu....  42.7 us
    unnamed x2, local copies, waits for them, and re-layouts  1.32 us

profile of v2, /device:TPU:0, one launch (start us, length us, event | category | flops | bytes accessed | tf_op | source)
XLA Modules:
  0.0 44.7 jit_solution(12428002374533366704)
XLA Ops:
  0.6 42.7 %shard_map.59 = (f32[8,64,128]{2,1,0:T(8,128)S(1)}, f32[64,128]{1,0:T(8,128)S(1)}) custom-call(f32[128,128]{1,0:T(8,128)} %rs_ref.1, f32[64,128]{1,0:T(8,128)} %bitcast.1, f32[128,128]{1,0:T(8,128)} %di_ref.1, bf16[64,4096]{1,0:T(8,128)(2,1)} %cov_ref.1), custom_call_target="tpu_custom_call" | custom-call | tf_op jit(solution)/shard_map/pallas_call | solution.py:190
  43.4 0.7 %copy.8 = f32[8,64,128]{2,1,0:T(8,128)} copy(f32[8,64,128]{2,1,0:T(8,128)S(1)} %get-tuple-element.2) | data formatting | bytes 524288
  44.1 0.6 %copy.9 = f32[64,128]{1,0:T(8,128)} copy(f32[64,128]{1,0:T(8,128)S(1)} %get-tuple-element.3) | data formatting | bytes 65536

commit v3 on v2

--- a/solution.py
+++ b/solution.py
@@ -14,6 +14,15 @@
 dot_exact = functools.partial(lax.dot_general, precision=lax.Precision.HIGHEST, preferred_element_type=F32)
 NN = (((1,), (0,)), ((), ()))
 NT = (((1,), (1,)), ((), ()))
+
+
+def halves(x):
+    high = x.astype(jnp.bfloat16)
+    return high, (x - high.astype(F32)).astype(jnp.bfloat16)
+
+
+def dot_low(a, b):
+    return lax.dot_general(a, b, NT, preferred_element_type=F32)
 
 
 def factor_inverse(gram):
@@ -58,8 +67,8 @@
 
 
 def kernel(n_row, n_col, rs_ref, fw_ref, di_ref, cov_ref, basis_ref, solved_ref,
-           cov32, tile, rows, solved_all, bases,
-           cov_send, cov_recv, f_send, f_fwd, f_recv, x_send, x_recv, b_send, b_recv):
+           cov_low, cov32, tile, rows, solved_all, bases, wide,
+           cov_load, cov_send, cov_recv, f_send, f_fwd, f_pass, f_recv, x_send, x_recv, x_fwd, x_other, b_send, b_recv):
     row = lax.axis_index("row")
     col = lax.axis_index("col")
     chips = n_col // CORES
@@ -68,7 +77,10 @@
     block = rs_ref.shape[0]
     width = fw_ref.shape[0]
     piece = cov32.shape[2]
-
+    out_rows = bases.shape[1]
+
+    load = pltpu.make_async_copy(cov_ref, cov_low, cov_load)
+    load.start()
     barrier = pltpu.get_barrier_semaphore()
     for d in range(1, n_row):
         pl.semaphore_signal(barrier, inc=1, device_id=(lax.rem(row + d, n_row), col), device_id_type=MESH)
@@ -78,8 +90,9 @@
     di = di_ref[...]
     rows[row, pl.ds(0, block), :] = dot_exact(rs_ref[...].T, di, NT)
     rows[row, pl.ds(block + col * width, width), :] = dot_exact(fw_ref[...], di, NT)
+    load.wait()
     for t in range(n_col):
-        cov32[t] = cov_ref[:, t * piece:(t + 1) * piece].astype(F32)
+        cov32[t] = cov_low[:, t * piece:(t + 1) * piece].astype(F32)
     pl.semaphore_wait(barrier, n_row + n_col - 2)
 
     def f_copy(source, target, send):
@@ -88,13 +101,23 @@
             src_ref=view, dst_ref=view, send_sem=send, recv_sem=f_recv.at[source],
             device_id=(row, target), device_id_type=MESH)
 
-    def far(d):
-        return lax.rem(chip + d, chips) * CORES + core
-
-    f_sends = [f_copy(col, far(d), f_send.at[d]) for d in range(1, chips)]
-    f_sends.append(f_copy(col, partner, f_send.at[0]))
-    for copy in f_sends:
-        copy.start()
+    quarter = chips // 4
+    inner = range(quarter, chips - quarter)
+    is_inner = (chip >= quarter) & (chip < chips - quarter)
+    outer = chip + quarter * (2 * (chip // (chips // 2)) - 1)
+
+    def to_outer(q):
+        return f_copy(q * CORES + core, outer * CORES + core, f_pass.at[q])
+
+    for q in inner:
+        @pl.when(chip != q)
+        def _():
+            f_copy(col, q * CORES + core, f_send.at[q]).start()
+    f_copy(col, partner, f_send.at[chips]).start()
+    if quarter:
+        @pl.when(is_inner)
+        def _():
+            f_copy(col, outer * CORES + core, f_send.at[chips + 1]).start()
 
     def cov_copy(source, target, d):
         return pltpu.make_async_remote_copy(
@@ -104,26 +127,44 @@
 
     order = sorted(range(1, n_col), key=lambda d: abs(2 * d - n_col))
     cov_sends = [cov_copy(col, lax.rem(col + d, n_col), d) for d in order]
-    for copy in cov_sends:
-        copy.start()
+    late = [is_inner & (lax.rem(col + d, n_col) // CORES == outer) for d in order]
+    for copy, wait in zip(cov_sends, late):
+        @pl.when(jnp.logical_not(wait))
+        def _():
+            copy.start()
     tile[col] = cov32[col]
 
-    forwards = []
-    for d in range(1, chips):
-        source = far(d)
-        f_copy(source, partner, f_fwd.at[d]).wait_recv()
-        copy = f_copy(source, partner, f_fwd.at[d])
-        copy.start()
-        forwards.append(copy)
-    for d in range(chips):
-        source = lax.rem(chip + d, chips) * CORES + (1 - core)
-        f_copy(source, partner, f_fwd.at[0]).wait_recv()
+    for q in range(chips):
+        @pl.when(chip != q)
+        def _():
+            f_copy(q * CORES + core, partner, f_fwd.at[q]).wait_recv()
+            if quarter:
+                @pl.when(is_inner & (outer != q))
+                def _():
+                    to_outer(q).start()
+            f_copy(q * CORES + core, partner, f_fwd.at[q]).start()
+    for copy, wait in zip(cov_sends, late):
+        @pl.when(wait)
+        def _():
+            copy.start()
+    for q in range(chips):
+        f_copy(q * CORES + (1 - core), partner, f_fwd.at[q]).wait_recv()
+
+    def x_half(i, part):
+        size = (i + 1) * block // CORES
+        return rows.at[i, pl.ds(pl.multiple_of(part * size, SUB), size)]
 
     def x_copy(i, target, d):
-        view = rows.at[i, pl.ds(0, (i + 1) * block)]
-        return pltpu.make_async_remote_copy(
-            src_ref=view, dst_ref=view, send_sem=x_send.at[d], recv_sem=x_recv.at[i],
+        return pltpu.make_async_remote_copy(
+            src_ref=x_half(i, core), dst_ref=x_half(i, core),
+            send_sem=x_send.at[d], recv_sem=x_recv.at[i],
             device_id=(target, col), device_id_type=MESH)
+
+    def x_pass(i, part):
+        return pltpu.make_async_remote_copy(
+            src_ref=x_half(i, part), dst_ref=x_half(i, part),
+            send_sem=x_fwd.at[i], recv_sem=x_other.at[i],
+            device_id=(row, partner), device_id_type=MESH)
 
     for i in range(n_row):
         @pl.when(row == i)
@@ -131,11 +172,17 @@
             for d in range(1, n_row):
                 x_copy(i, (i + d) % n_row, d).start()
 
+    for i in range(n_row):
+        @pl.when(row != i)
+        def _():
+            x_copy(i, (i + 1) % n_row, 0).wait_recv()
+            x_pass(i, core).start()
+
     solved = []
     for i in range(n_row):
         @pl.when(row != i)
         def _():
-            x_copy(i, (i + 1) % n_row, 0).wait_recv()
+            x_pass(i, 1 - core).wait_recv()
 
         value = rows[i, pl.ds(0, block), :]
         if i:
@@ -150,9 +197,9 @@
         cov_copy(lax.rem(col + d, n_col), col, d).wait_recv()
     whole = tile[...].reshape(n_col * width, piece).astype(jnp.bfloat16)
     weighted = lax.dot_general(solved_low, whole, NN, preferred_element_type=F32)
+    wide[...] = weighted.T
     inverse = factor_inverse(dot_exact(weighted, weighted, NT))
-    basis = dot_exact(weighted.T, inverse, NT)
-    bases[...] = basis.reshape(bases.shape)
+    inverse_high, inverse_low = halves(inverse)
 
     def b_copy(source, target, d):
         return pltpu.make_async_remote_copy(
@@ -160,17 +207,53 @@
             send_sem=b_send.at[d], recv_sem=b_recv.at[source],
             device_id=(row, target), device_id_type=MESH)
 
-    b_sends = [b_copy(col, lax.rem(col + d, n_col), d) for d in order]
-    for copy in b_sends:
-        copy.start()
-    basis_ref[col] = bases[col]
-    for copy in f_sends + forwards + cov_sends:
+    def basis_rows(targets):
+        taken = jnp.concatenate([wide[pl.ds(pl.multiple_of(t * out_rows, out_rows), out_rows), :] for t in targets], axis=0)
+        high, low = halves(taken)
+        found = dot_low(high, inverse_high) + (dot_low(high, inverse_low) + dot_low(low, inverse_high))
+        return [found[j * out_rows:(j + 1) * out_rows, :] for j in range(len(targets))]
+
+    b_sends = []
+    half = n_col // 2
+    for chosen in (order[:half], order[half:]):
+        targets = [lax.rem(col + d, n_col) for d in chosen]
+        found = basis_rows(targets if len(chosen) == half else targets + [col])
+        for d, target, value in zip(chosen, targets, found):
+            bases[target] = value
+        for d, target in zip(chosen, targets):
+            copy = b_copy(col, target, d)
+            copy.start()
+            b_sends.append(copy)
+        if len(found) > len(chosen):
+            basis_ref[col] = found[-1]
+    for copy in cov_sends:
         copy.wait_send()
+    for q in inner:
+        @pl.when(chip != q)
+        def _():
+            f_copy(col, q * CORES + core, f_send.at[q]).wait_send()
+    f_copy(col, partner, f_send.at[chips]).wait_send()
+    if quarter:
+        @pl.when(is_inner)
+        def _():
+            f_copy(col, outer * CORES + core, f_send.at[chips + 1]).wait_send()
+    for q in range(chips):
+        @pl.when(chip != q)
+        def _():
+            f_copy(q * CORES + core, partner, f_fwd.at[q]).wait_send()
+            if quarter:
+                @pl.when(is_inner & (outer != q))
+                def _():
+                    to_outer(q).wait_send()
     for i in range(n_row):
         @pl.when(row == i)
         def _():
             for d in range(1, n_row):
                 x_copy(i, (i + d) % n_row, d).wait_send()
+
+        @pl.when(row != i)
+        def _():
+            x_pass(i, core).wait_send()
     for d in order:
         b_copy(lax.rem(col + d, n_col), col, d).wait_recv()
     for copy in b_sends:
@@ -193,17 +276,19 @@
                 pltpu.VMEM((n_col, out_rows, rank), F32),
                 pltpu.VMEM((width, rank), F32),
             ),
-            in_specs=[vmem] * 4,
+            in_specs=[vmem] * 3 + [pl.BlockSpec(memory_space=pl.ANY)],
             out_specs=(vmem, vmem),
             scratch_shapes=[
+                pltpu.VMEM(phase_cov.shape, phase_cov.dtype),
                 pltpu.VMEM((n_col, width, piece), F32),
                 pltpu.VMEM((n_col, width, piece), F32),
                 pltpu.VMEM((n_row, (n_row + 1) * block, rank), F32),
                 pltpu.VMEM((n_row * block, rank), F32),
                 pltpu.VMEM((n_col, out_rows, rank), F32),
-                dma((n_col,)), dma((n_col,)),
-                dma((n_col,)), dma((n_col,)), dma((n_col,)),
-                dma((n_row,)), dma((n_row,)),
+                pltpu.VMEM((piece, rank), F32),
+                dma, dma((n_col,)), dma((n_col,)),
+                dma((n_col + 2,)), dma((n_col,)), dma((n_col,)), dma((n_col,)),
+                dma((n_row,)), dma((n_row,)), dma((n_row,)), dma((n_row,)),
                 dma((n_col,)), dma((n_col,)),
             ],
             compiler_params=pltpu.CompilerParams(collective_id=0, has_side_effects=True),

time: 44.8 us -> 43 us (0.960)
  Pallas kernels: 42.7 us -> 40.8 us
    pallas_call x1, Pallas kernels: 42.7 us -> 40.8 us  [local(): pl.pallas_call(functools.partial(kernel, n_row, n_col), out_shape=(pltpu....]
where the time goes in v3:
time: 43 us; the launch traced here: 42.8 us
  Pallas kernels  40.8 us (95%)
  local copies, waits for them, and re-layouts  1.32 us (3%)
  between operations  0.64 us (1%)
    pallas_call x1, Pallas kernels, local(): pl.pallas_call(functools.partial(kernel, n_row, n_col), out_shape=(pltpu....  40.8 us
    unnamed x2, local copies, waits for them, and re-layouts  1.32 us

profile of v3, /device:TPU:0, one launch (start us, length us, event | category | flops | bytes accessed | tf_op | source)
XLA Modules:
  0.0 42.8 jit_solution(12051195950905731886)
XLA Ops:
  0.6 40.8 %shard_map.59 = (f32[8,64,128]{2,1,0:T(8,128)S(1)}, f32[64,128]{1,0:T(8,128)S(1)}) custom-call(f32[128,128]{1,0:T(8,128)} %rs_ref.1, f32[64,128]{1,0:T(8,128)} %bitcast.1, f32[128,128]{1,0:T(8,128)} %di_ref.1, bf16[64,4096]{1,0:T(8,128)(2,1)} %cov_ref.1), custom_call_target="tpu_custom_call" | custom-call | tf_op jit(solution)/shard_map/pallas_call | solution.py:273
  41.5 0.7 %copy.8 = f32[8,64,128]{2,1,0:T(8,128)} copy(f32[8,64,128]{2,1,0:T(8,128)S(1)} %get-tuple-element.2) | data formatting | bytes 524288
  42.2 0.6 %copy.9 = f32[64,128]{1,0:T(8,128)} copy(f32[64,128]{1,0:T(8,128)S(1)} %get-tuple-element.3) | data formatting | bytes 65536
